TPU v7x, 32 devices: a whole 2x2x4 slice. The times are simulated.
32 devices in a mesh: dp: 8 (over y, x, core), tensor: 4 (over z).
Axes of the slice: x: 2, y: 2, z: 4, core: 2. Of those that a mesh axis runs over, the one named last changes fastest.
Arguments:
- x_in: bfloat16 [16384, 1024], P(('dp', 'tensor')), may hold values from -6 to 6
- in_w: bfloat16 [1024, 3, 1024], P('dp', None, 'tensor'), may hold values from -0.1875 to 0.1875
- out_w: bfloat16 [1024, 1024], P('tensor', 'dp'), may hold values from -0.1875 to 0.1875
- gate_w: bfloat16 [1024, 4608], P('dp', 'tensor'), may hold values from -0.1875 to 0.1875
- up_w: bfloat16 [1024, 4608], P('dp', 'tensor'), may hold values from -0.1875 to 0.1875
- down_w: bfloat16 [4608, 1024], P('tensor', 'dp'), may hold values from -0.125 to 0.125
- conv_w: bfloat16 [3, 1024], replicated, may hold values from -3 to 3
- gain1: bfloat16 [1024], replicated, may hold values from 0.25 to 1.75
- gain2: bfloat16 [1024], replicated, may hold values from 0.25 to 1.75
- d_out: bfloat16 [16384, 1024], P(('dp', 'tensor')), may hold values from -6 to 6
Outputs:
- block_out: bfloat16 [16384, 1024], P(('dp', 'tensor'))
- d_x: bfloat16 [16384, 1024], P(('dp', 'tensor'))
- grad_in: float32 [1024, 3, 1024], P('dp', None, 'tensor')
- grad_out: float32 [1024, 1024], P('tensor', 'dp')
- grad_gate: float32 [1024, 4608], P('dp', 'tensor')
- grad_up: float32 [1024, 4608], P('dp', 'tensor')
- grad_down: float32 [4608, 1024], P('tensor', 'dp')
- grad_conv: float32 [3, 1024], replicated
- grad_gain1: float32 [1024], replicated
- grad_gain2: float32 [1024], replicated
All inputs are finite; a program needn't handle non-finite values.
Results may differ from a plain program's by a relative error of at most 0.018.
Values may be sent and summed in bfloat16 or wider, within the bound.
No kernel may reach another device: no remote copies, remote signals or barrier semaphores. Data moves between devices by JAX's collectives and lax.ppermute only.
A program may use at most 192 MiB of HBM per device.

v0:
```python
import jax
import jax.numpy as jnp
from jax import lax
from jax.sharding import PartitionSpec as P

LEN = 1024
epsilon = 1e-05


def in_blocks(x, dim, devices):
    before, after = (x.shape[:dim], x.shape[dim + 1 :])
    return jnp.moveaxis(x.reshape(*before, devices, -1, *after), dim, 0)


def sum_at_owner(x, axis, dim):
    tiles = in_blocks(x, dim, lax.axis_size(axis))
    arrived = lax.all_to_all(tiles, axis, split_axis=0, concat_axis=0, tiled=True)
    return arrived.astype(jnp.float32).sum(axis=0)


def norm_rows(values):
    scale = lax.rsqrt(jnp.mean(values * values, axis=-1, keepdims=True) + epsilon)
    return (values * scale, scale)


def norm_back(grad_h, normed, scale, gain):
    grad_n = grad_h * gain
    inner = jnp.mean(grad_n * normed, axis=-1, keepdims=True)
    return scale * (grad_n - normed * inner)


def delayed(values, steps_back):
    length = values.shape[1]
    padded = jnp.pad(values, ((0, 0), (steps_back, 0), (0, 0)))
    return padded[:, :length]


def advanced(values, steps_ahead):
    padded = jnp.pad(values, ((0, 0), (0, steps_ahead), (0, 0)))
    return padded[:, steps_ahead:]


def body(x_in, in_w, out_w, gate_w, up_w, down_w, conv_w, gain1, gain2, d_out):
    in_full, out_full, gate_full, up_full, down_full = (
        lax.all_gather(in_w, "dp", axis=0, tiled=True),
        lax.all_gather(out_w, "dp", axis=1, tiled=True),
        lax.all_gather(gate_w, "dp", axis=0, tiled=True),
        lax.all_gather(up_w, "dp", axis=0, tiled=True),
        lax.all_gather(down_w, "dp", axis=1, tiled=True),
    )
    model_width = x_in.shape[1]
    width = out_full.shape[0]
    offset = lax.axis_index("tensor") * width
    kernel = lax.dynamic_slice_in_dim(conv_w, offset, width, 1).astype(jnp.float32)
    gain_one = gain1.astype(jnp.float32)
    gain_two = gain2.astype(jnp.float32)
    tokens = x_in.astype(jnp.float32)
    normed_one, scale_one = norm_rows(tokens)
    first = (normed_one * gain_one).astype(jnp.bfloat16)
    first_all = lax.all_gather(first, "tensor", axis=0, tiled=True)
    group_rows = first_all.shape[0]
    seq_count = group_rows // LEN
    projected = jnp.einsum("td,dkc->tkc", first_all, in_full, preferred_element_type=jnp.float32)
    b_part = projected[:, 0].reshape(seq_count, LEN, width)
    c_part = projected[:, 1].reshape(seq_count, LEN, width)
    x_part = projected[:, 2].reshape(seq_count, LEN, width)
    mixed_in = b_part * x_part
    back_one = delayed(mixed_in, 1)
    back_two = delayed(mixed_in, 2)
    conv_out = kernel[2] * mixed_in + kernel[1] * back_one + kernel[0] * back_two
    branch = (c_part * conv_out).reshape(group_rows, width).astype(jnp.bfloat16)
    rows_now = branch
    mixed = lax.psum_scatter(
        jnp.dot(rows_now, out_full, preferred_element_type=jnp.float32).astype(jnp.bfloat16),
        "tensor",
        scatter_dimension=0,
        tiled=True,
    ).astype(jnp.float32)
    resid = tokens + mixed
    normed_two, scale_two = norm_rows(resid)
    second = (normed_two * gain_two).astype(jnp.bfloat16)
    second_all = lax.all_gather(second, "tensor", axis=0, tiled=True)
    gate = jnp.dot(second_all, gate_full, preferred_element_type=jnp.float32)
    up_val = jnp.dot(second_all, up_full, preferred_element_type=jnp.float32)
    sigma = jax.nn.sigmoid(gate)
    silu_gate = gate * sigma
    hidden = (silu_gate * up_val).astype(jnp.bfloat16)
    rows_now = hidden
    ffn = lax.psum_scatter(
        jnp.dot(rows_now, down_full, preferred_element_type=jnp.float32).astype(jnp.bfloat16),
        "tensor",
        scatter_dimension=0,
        tiled=True,
    ).astype(jnp.float32)
    block_out = (resid + ffn).astype(jnp.bfloat16)
    cot_all = lax.all_gather(d_out, "tensor", axis=0, tiled=True)
    d_hidden = jnp.einsum("td,fd->tf", cot_all, down_full, preferred_element_type=jnp.float32)
    d_gate = (d_hidden * up_val * sigma * (1.0 + gate * (1.0 - sigma))).astype(jnp.bfloat16)
    d_up = (d_hidden * silu_gate).astype(jnp.bfloat16)
    grad_down = jnp.einsum("tf,td->fd", hidden, cot_all, preferred_element_type=jnp.float32)
    grad_gate = jnp.einsum("td,tf->df", second_all, d_gate, preferred_element_type=jnp.float32)
    grad_up = jnp.einsum("td,tf->df", second_all, d_up, preferred_element_type=jnp.float32)
    grad_gate, grad_up, grad_down = (
        lax.psum_scatter(grad_gate, "dp", scatter_dimension=0, tiled=True),
        lax.psum_scatter(grad_up, "dp", scatter_dimension=0, tiled=True),
        lax.psum_scatter(grad_down, "dp", scatter_dimension=1, tiled=True),
    )
    part_gate = jnp.einsum("tf,df->td", d_gate, gate_full, preferred_element_type=jnp.float32)
    part_up = jnp.einsum("tf,df->td", d_up, up_full, preferred_element_type=jnp.float32)
    d_second = lax.psum_scatter(
        (part_gate + part_up).astype(jnp.bfloat16), "tensor", scatter_dimension=0, tiled=True
    ).astype(jnp.float32)
    gain_two_part = jnp.sum(d_second * normed_two, axis=0)
    d_resid = d_out.astype(jnp.float32) + norm_back(d_second, normed_two, scale_two, gain_two)
    d_mixed = lax.all_gather(d_resid.astype(jnp.bfloat16), "tensor", axis=0, tiled=True)
    grad_out = jnp.einsum("tc,td->cd", branch, d_mixed, preferred_element_type=jnp.float32)
    d_branch = jnp.einsum(
        "td,cd->tc", d_mixed, out_full, preferred_element_type=jnp.float32
    ).reshape(seq_count, LEN, width)
    d_conv = d_branch * c_part
    d_c = d_branch * conv_out
    d_mixin = kernel[2] * d_conv + kernel[1] * advanced(d_conv, 1) + kernel[0] * advanced(d_conv, 2)
    tap_two = jnp.sum(d_conv * mixed_in, axis=(0, 1))
    tap_one = jnp.sum(d_conv * back_one, axis=(0, 1))
    tap_zero = jnp.sum(d_conv * back_two, axis=(0, 1))
    d_b = d_mixin * x_part
    d_xpart = d_mixin * b_part
    d_proj = (
        jnp.stack([d_b, d_c, d_xpart], axis=2).reshape(group_rows, 3, width).astype(jnp.bfloat16)
    )
    grad_in = jnp.einsum("td,tkc->dkc", first_all, d_proj, preferred_element_type=jnp.float32)
    grad_in, grad_out = (
        sum_at_owner(grad_in.astype(jnp.bfloat16), "dp", 0),
        sum_at_owner(grad_out.astype(jnp.bfloat16), "dp", 1),
    )
    rows_now = d_proj
    d_first = lax.psum_scatter(
        jnp.einsum("tkc,dkc->td", rows_now, in_full, preferred_element_type=jnp.float32).astype(
            jnp.bfloat16
        ),
        "tensor",
        scatter_dimension=0,
        tiled=True,
    ).astype(jnp.float32)
    gain_one_part = jnp.sum(d_first * normed_one, axis=0)
    d_x = (d_resid + norm_back(d_first, normed_one, scale_one, gain_one)).astype(jnp.bfloat16)
    taps_local = jnp.stack([tap_zero, tap_one, tap_two], axis=0)
    taps_whole = lax.dynamic_update_slice_in_dim(
        jnp.zeros((3, model_width), jnp.float32), taps_local, offset, 1
    )
    grad_gain1, grad_gain2, grad_conv = lax.psum(
        (gain_one_part, gain_two_part, taps_whole), ("dp", "tensor")
    )
    return (
        block_out,
        d_x,
        grad_in,
        grad_out,
        grad_gate,
        grad_up,
        grad_down,
        grad_conv,
        grad_gain1,
        grad_gain2,
    )


def solution(mesh):
    in_specs = (
        P(("dp", "tensor"), None),
        P("dp", None, "tensor"),
        P("tensor", "dp"),
        P("dp", "tensor"),
        P("dp", "tensor"),
        P("tensor", "dp"),
        P(),
        P(),
        P(),
        P(("dp", "tensor"), None),
    )
    out_specs = (
        P(("dp", "tensor"), None),
        P(("dp", "tensor"), None),
        P("dp", None, "tensor"),
        P("tensor", "dp"),
        P("dp", "tensor"),
        P("dp", "tensor"),
        P("tensor", "dp"),
        P(),
        P(),
        P(),
    )
    return jax.shard_map(body, mesh=mesh, in_specs=in_specs, out_specs=out_specs, check_vma=False)
```

profile of v0, /device:TPU:0, one launch (start us, length us, event | category | flops | bytes accessed | tf_op | source)
XLA Modules:
  0.0 1019.6 jit_solution(11951078540977682232)
XLA Ops:
  8.6 1.5 fusion.26
  10.2 2.5 fusion.23
  13.5 12.6 %all_gather.29 = bf16[256,1024]{1,0:T(8,128)(2,1)S(1)} all-gather(bf16[256,128]{1,0:T(8,128)(2,1)S(1)} %copy-done.21), channel_id=1, replica_groups=mesh['dp'=8,'tensor'=4] {'dp'}, dimensions={1}, use_global_device_ids=true | all-gather | bytes 589824 | tf_op jit(solution)/shard_map/all_gather | solution.py:46
  26.1 12.9 %all-gather.11.cloned.1.call-done = bf16[1024,3,256]{2,0,1:T(8,128)(2,1)} async-done(((bf16[128,3,256]{2,0,1:T(8,128)(2,1)}), bf16[1024,3,256]{2,0,1:T(8,128)(2,1)}) %all-gather.11.cloned.1.call-update) | async-done | bytes 1572880 | tf_op jit(solution)/shard_map/all_gather | solution.py:45
  39.0 82.9 %all-gather.9.cloned.1.call-done = bf16[2048,1024]{1,0:T(8,128)(2,1)} async-done(((bf16[512,1024]{1,0:T(8,128)(2,1)}), bf16[2048,1024]{1,0:T(8,128)(2,1)}) %all-gather.9.cloned.1.call-update) | async-done | bytes 4194320 | tf_op jit(solution)/shard_map/all_gather | solution.py:60
  122.0 5.6 fusion.3
  128.1 2.2 copy-done.14
  132.9 2.1 multiply_convert_fusion.7
  136.0 3.3 convolution_convert_fusion.1
  140.1 74.8 %reduce-scatter.8.cloned.1.call-done = bf16[512,1024]{1,0:T(8,128)(2,1)} async-done(((bf16[2048,1024]{1,0:T(8,128)(2,1)}), bf16[512,1024]{1,0:T(8,128)(2,1)}) %reduce-scatter.8.cloned.1.call-update) | async-done | bytes 1048592 | tf_op jit(solution)/shard_map/reduce_scatter | solution.py:73
  214.8 1.7 multiply_reduce_fusion.2
  216.6 1.4 multiply_convert_fusion.6
  220.6 25.7 %all-gather.15.cloned.1.call-done = bf16[1024,1152]{1,0:T(8,128)(2,1)} async-done(((bf16[128,1152]{1,0:T(8,128)(2,1)}), bf16[1024,1152]{1,0:T(8,128)(2,1)}) %all-gather.15.cloned.1.call-update) | async-done | bytes 2359312 | tf_op jit(solution)/shard_map/all_gather | solution.py:47
  246.3 82.9 %all-gather.13.cloned.1.call-done = bf16[2048,1024]{1,0:T(8,128)(2,1)} async-done(((bf16[512,1024]{1,0:T(8,128)(2,1)}), bf16[2048,1024]{1,0:T(8,128)(2,1)}) %all-gather.13.cloned.1.call-update) | async-done | bytes 4194320 | tf_op jit(solution)/shard_map/all_gather | solution.py:82
  329.2 10.3 %fusion.39 = f32[2048,1152]{1,0:T(8,128)} fusion(bf16[2048,1024]{1,0:T(8,128)(2,1)} %all-gather.13.cloned.1.call-done, bf16[1024,1152]{1,0:T(8,128)(2,1)} %all-gather.15.cloned.1.call-done), kind=kOutput, calls=%fused_computation.77 | convolution fusion | flops 4831838208 | bytes 15990784 | tf_op jit(solution)/shard_map/dot_general | solution.py:83
  339.4 19.2 %all-gather.17.cloned.1.call-done = bf16[1024,1152]{1,0:T(8,128)(2,1)} async-done(((bf16[128,1152]{1,0:T(8,128)(2,1)}), bf16[1024,1152]{1,0:T(8,128)(2,1)}) %all-gather.17.cloned.1.call-update) | async-done | bytes 2359312 | tf_op jit(solution)/shard_map/all_gather | solution.py:48
  358.6 10.3 %fusion.40 = f32[2048,1152]{1,0:T(8,128)} fusion(bf16[2048,1024]{1,0:T(8,128)(2,1)} %all-gather.13.cloned.1.call-done, bf16[1024,1152]{1,0:T(8,128)(2,1)} %all-gather.17.cloned.1.call-done), kind=kOutput, calls=%fused_computation.78 | convolution fusion | flops 4831838208 | bytes 15990784 | tf_op jit(solution)/shard_map/dot_general | solution.py:84
  368.9 21.1 %all-gather.19.cloned.1.call-done = bf16[1152,1024]{1,0:T(8,128)(2,1)} async-done(((bf16[1152,128]{1,0:T(8,128)(2,1)}), bf16[1152,1024]{1,0:T(8,128)(2,1)}) %all-gather.19.cloned.1.call-update) | async-done | bytes 2359312 | tf_op jit(solution)/shard_map/all_gather | solution.py:49
  390.1 82.4 %all-gather.21.cloned.1.call-done = bf16[2048,1024]{1,0:T(8,128)(2,1)} async-done(((bf16[512,1024]{1,0:T(8,128)(2,1)}), bf16[2048,1024]{1,0:T(8,128)(2,1)}) %all-gather.21.cloned.1.call-update) | async-done | bytes 4194320 | tf_op jit(solution)/shard_map/all_gather | solution.py:96
  472.5 17.8 %multiply_convert_fusion = (bf16[2048,1152]{1,0:T(8,128)(2,1)}, bf16[2048,1152]{1,0:T(8,128)(2,1)}, bf16[2048,1152]{1,0:T(8,128)(2,1)}) fusion(f32[2048,1152]{1,0:T(8,128)} %fusion.39, f32[2048,1152]{1,0:T(8,128)} %fusion.40, bf16[2048,1024]{1,0:T(8,128)(2,1)} %all-gather.21.cloned.1.call-done, bf16[1152,1024]{1,0:T(8,128)(2,1)} %all-gather.19.cloned.1.call-done), kind=kOutput, calls=%fused_computation | convolution fusion | flops 4867227648 | bytes 39583744 | tf_op jit(solution)/shard_map/td,fd->tf/dot_general | solution.py:97
  490.4 7.7 fusion.41
  498.0 7.7 add_convert_fusion
  505.9 75.4 %reduce-scatter.12.cloned.1.call-done = bf16[512,1024]{1,0:T(8,128)(2,1)} async-done(((bf16[2048,1024]{1,0:T(8,128)(2,1)}), bf16[512,1024]{1,0:T(8,128)(2,1)}) %reduce-scatter.12.cloned.1.call-update) | async-done | bytes 1048592 | tf_op jit(solution)/shard_map/reduce_scatter | solution.py:110
  581.3 2.2 fusion.22
  583.5 1.8 fusion.35
  585.4 81.4 %all-gather.23.cloned.1.call-done = bf16[2048,1024]{1,0:T(8,128)(2,1)} async-done(((bf16[512,1024]{1,0:T(8,128)(2,1)}), bf16[2048,1024]{1,0:T(8,128)(2,1)}) %all-gather.23.cloned.1.call-update) | async-done | bytes 4194320 | tf_op jit(solution)/shard_map/all_gather | solution.py:115
  666.7 5.8 fusion.27
  677.5 5.0 bitcast_convert_fusion
  682.5 9.5 convolution_convert_fusion
  692.1 10.5 %fusion.42 = f32[1024,1152]{1,0:T(8,128)} fusion(bf16[2048,1024]{1,0:T(8,128)(2,1)} %all-gather.13.cloned.1.call-done, bf16[2048,1152]{1,0:T(8,128)(2,1)} %get-tuple-element.25), kind=kOutput, calls=%fused_computation.80 | convolution fusion | flops 4831838208 | bytes 13631488 | tf_op jit(solution)/shard_map/td,tf->df/dot_general | solution.py:101
  702.6 10.3 %fusion.43 = f32[1024,1152]{1,0:T(8,128)} fusion(bf16[2048,1024]{1,0:T(8,128)(2,1)} %all-gather.13.cloned.1.call-done, bf16[2048,1152]{1,0:T(8,128)(2,1)} %get-tuple-element.24), kind=kOutput, calls=%fused_computation.81 | convolution fusion | flops 4831838208 | bytes 13631488 | tf_op jit(solution)/shard_map/td,tf->df/dot_general | solution.py:102
  713.0 9.8 fusion.44
  722.8 3.8 fusion.32
  727.5 4.4 all-to-all-start.1
  731.9 6.7 fusion.29
  738.6 1.3 copy.22
  739.9 1.8 all-to-all-done.1
  741.7 4.3 all-to-all-start
  746.1 1.8 convert_reduce_fusion.1
  747.9 19.2 %all-to-all-done = bf16[8,128,3,256]{3,1,2,0:T(8,128)(2,1)} async-done(((bf16[8,128,3,256]{3,1,2,0:T(8,128)(2,1)}), bf16[8,128,3,256]{3,1,2,0:T(8,128)(2,1)}, u32[]{:S(2)}, u32[]{:S(2)}) %all-to-all-start) | async-done | bytes 1572896 | tf_op jit(solution)/shard_map/all_to_all | solution.py:17
  767.1 2.5 convert_reduce_fusion
  769.6 2.0 fusion.25
  771.6 42.7 %all-reduce.4 = (f32[3,1024]{1,0:T(4,128)}, f32[1024]{0:T(1024)}, f32[1024]{0:T(1024)}) all-reduce(f32[3,1024]{1,0:T(4,128)S(1)} %maximum_dynamic-update-slice_fusion, f32[1024]{0:T(1024)S(1)} %get-tuple-element.14, f32[1024]{0:T(1024)S(1)} %get-tuple-element.12), channel_id=1, replica_groups=mesh['dp'=8,'tensor'=4] {'dp','tensor'}, use_global_device_ids=true, to_apply=%region_16.17 | all-reduce | flops 5120 | bytes 40960 | tf_op jit(solution)/shard_map/psum | solution.py:151
  814.3 24.2 %reduce-scatter.10.cloned.1.call-done = bf16[512,1024]{1,0:T(8,128)(2,1)} async-done(((bf16[2048,1024]{1,0:T(8,128)(2,1)}), bf16[512,1024]{1,0:T(8,128)(2,1)}) %reduce-scatter.10.cloned.1.call-update) | async-done | bytes 1048592 | tf_op jit(solution)/shard_map/reduce_scatter | solution.py:89
  838.5 4.1 fusion.18
  842.7 54.2 %reduce-scatter.16.cloned.1.call-done = f32[128,1152]{1,0:T(8,128)} async-done(((f32[1024,1152]{1,0:T(8,128)}), f32[128,1152]{1,0:T(8,128)}) %reduce-scatter.16.cloned.1.call-update) | async-done | bytes 589840 | tf_op jit(solution)/shard_map/reduce_scatter | solution.py:104
  896.9 58.2 %reduce-scatter.18.cloned.1.call-done = f32[128,1152]{1,0:T(8,128)} async-done(((f32[1024,1152]{1,0:T(8,128)}), f32[128,1152]{1,0:T(8,128)}) %reduce-scatter.18.cloned.1.call-update) | async-done | bytes 589840 | tf_op jit(solution)/shard_map/reduce_scatter | solution.py:105
  955.1 57.8 %reduce-scatter.20.cloned.1.call-done = f32[1152,128]{1,0:T(8,128)} async-done(((f32[1152,1024]{1,0:T(8,128)}), f32[1152,128]{1,0:T(8,128)}) %reduce-scatter.20.cloned.1.call-update) | async-done | bytes 589840 | tf_op jit(solution)/shard_map/reduce_scatter | solution.py:106
  (104 shorter events, 15.8 us)
Async XLA Ops:
  7.2 31.9 %all-gather.11.cloned.1.call-start = ((), (), s32[]{:S(2)}) async-start(), calls=%async_computation.10 | async-start | bytes 1769472 | tf_op jit(solution)/shard_map/all_gather | solution.py:45
  7.9 114.1 %all-gather.9.cloned.1.call-start = ((), (), s32[]{:S(2)}) async-start(), calls=%async_computation.9 | async-start | bytes 5242880 | tf_op jit(solution)/shard_map/all_gather | solution.py:60
  8.6 4.8 copy-start.19
  8.6 4.8 copy-start.21
  10.2 111.8 %copy-start.22 = (f32[512]{0:T(512)}, f32[512]{0:T(512)S(1)}, u32[]{:S(2)}) copy-start(f32[512]{0:T(512)S(1)} %add_rsqrt_fusion.1) | copy-start | bytes 6148
  12.7 202.1 %reduce-scatter.8.cloned.1.call-start = ((), (), s32[]{:S(2)}) async-start(), calls=%async_computation.11 | async-start | bytes 5242880 | tf_op jit(solution)/shard_map/reduce_scatter | solution.py:73
  26.1 108.9 %copy-start.15 = (bf16[256,1024]{1,0:T(8,128)(2,1)}, bf16[256,1024]{1,0:T(8,128)(2,1)S(1)}, u32[]{:S(2)}) copy-start(bf16[256,1024]{1,0:T(8,128)(2,1)S(1)} %all_gather.29) | copy-start | bytes 1572868
  127.6 2.7 copy-start.14
  130.3 1.3 copy-start.2
  130.3 2.0 copy-start.6
  130.3 2.6 copy-start.8
  132.3 2.8 copy-start.4
  135.0 1.0 copy-start.13
  139.4 0.7 copy-start.24
  139.4 75.5 %copy-start = (bf16[512,1024]{1,0:T(8,128)(2,1)S(1)}, bf16[512,1024]{1,0:T(8,128)(2,1)}, u32[]{:S(2)}) copy-start(bf16[512,1024]{1,0:T(8,128)(2,1)} %param.10) | copy-start | bytes 3145732
  139.4 106.9 %all-gather.15.cloned.1.call-start = ((), (), s32[]{:S(2)}) async-start(), calls=%async_computation.13 | async-start | bytes 2654208 | tf_op jit(solution)/shard_map/all_gather | solution.py:47
  140.0 189.2 %all-gather.13.cloned.1.call-start = ((), (), s32[]{:S(2)}) async-start(), calls=%async_computation.12 | async-start | bytes 5242880 | tf_op jit(solution)/shard_map/all_gather | solution.py:82
  214.8 1.7 copy-start.1
  218.0 140.7 %all-gather.17.cloned.1.call-start = ((), (), s32[]{:S(2)}) async-start(), calls=%async_computation.14 | async-start | bytes 2654208 | tf_op jit(solution)/shard_map/all_gather | solution.py:48
  218.6 171.5 %all-gather.19.cloned.1.call-start = ((), (), s32[]{:S(2)}) async-start(), calls=%async_computation.15 | async-start | bytes 2654208 | tf_op jit(solution)/shard_map/all_gather | solution.py:49
  219.3 253.2 %all-gather.21.cloned.1.call-start = ((), (), s32[]{:S(2)}) async-start(), calls=%async_computation.17 | async-start | bytes 5242880 | tf_op jit(solution)/shard_map/all_gather | solution.py:96
  220.1 361.2 %reduce-scatter.12.cloned.1.call-start = ((), (), s32[]{:S(2)}) async-start(), calls=%async_computation.18 | async-start | bytes 5242880 | tf_op jit(solution)/shard_map/reduce_scatter | solution.py:110
  472.5 17.8 %copy-start.25 = (bf16[1024,1152]{1,0:T(8,128)(2,1)S(1)}, bf16[1024,1152]{1,0:T(8,128)(2,1)}, u32[]{:S(2)}) copy-start(bf16[1024,1152]{1,0:T(8,128)(2,1)} %all-gather.15.cloned.1.call-done) | copy-start | bytes 7077892
  490.3 7.7 copy-start.26
  490.3 7.7 copy-start.28
  505.8 77.7 %copy-start.10 = (bf16[512,1024]{1,0:T(8,128)(2,1)S(1)}, bf16[512,1024]{1,0:T(8,128)(2,1)}, u32[]{:S(2)}) copy-start(bf16[512,1024]{1,0:T(8,128)(2,1)} %param.19) | copy-start | bytes 3145732
  505.8 160.9 %all-gather.23.cloned.1.call-start = ((), (), s32[]{:S(2)}) async-start(), calls=%async_computation.19 | async-start | bytes 5242880 | tf_op jit(solution)/shard_map/all_gather | solution.py:115
  581.3 2.2 copy-start.11
  585.3 184.2 %reduce-scatter.14.cloned.1.call-start = ((), (), s32[]{:S(2)}) async-start(), calls=%async_computation.20 | async-start | bytes 5242880 | tf_op jit(solution)/shard_map/reduce_scatter | solution.py:137
  666.7 5.8 copy-start.5
  666.7 5.8 copy-start.9
  666.7 6.0 copy-start.12
  672.8 1.6 copy-start.3
  673.6 2.8 copy-start.16
  674.4 1.6 copy-start.7
  675.1 1.3 copy-start.18
  676.0 1.5 copy-start.27
  676.4 1.0 copy-start.17
  682.5 156.0 %reduce-scatter.10.cloned.1.call-start = ((), (), s32[]{:S(2)}) async-start(), calls=%async_computation.16 | async-start | bytes 5242880 | tf_op jit(solution)/shard_map/reduce_scatter | solution.py:89
  692.0 204.9 %reduce-scatter.16.cloned.1.call-start = ((), (), s32[]{:S(2)}) async-start(), calls=%async_computation.21 | async-start | bytes 5308416 | tf_op jit(solution)/shard_map/reduce_scatter | solution.py:104
  702.6 252.5 %reduce-scatter.18.cloned.1.call-start = ((), (), s32[]{:S(2)}) async-start(), calls=%async_computation.22 | async-start | bytes 5308416 | tf_op jit(solution)/shard_map/reduce_scatter | solution.py:105
  713.0 299.9 %reduce-scatter.20.cloned.1.call-start = ((), (), s32[]{:S(2)}) async-start(), calls=%async_computation.23 | async-start | bytes 5308416 | tf_op jit(solution)/shard_map/reduce_scatter | solution.py:106
  727.5 14.2 %all-to-all-start.1 = ((bf16[8,256,128]{2,1,0:T(8,128)(2,1)}), bf16[8,256,128]{2,1,0:T(8,128)(2,1)}, u32[]{:S(2)}, u32[]{:S(2)}) async-start(bf16[8,256,128]{2,1,0:T(8,128)(2,1)} %bitcast.76), calls=%async_computation.5 | async-start | bytes 1048576 | tf_op jit(solution)/shard_map/all_to_all | solution.py:17
  741.7 25.4 %all-to-all-start = ((bf16[8,128,3,256]{3,1,2,0:T(8,128)(2,1)}), bf16[8,128,3,256]{3,1,2,0:T(8,128)(2,1)}, u32[]{:S(2)}, u32[]{:S(2)}) async-start(bf16[8,128,3,256]{3,1,2,0:T(8,128)(2,1)} %copy.22), calls=%async_computation.4 | async-start | bytes 3145728 | tf_op jit(solution)/shard_map/all_to_all | solution.py:17
  746.0 23.5 %copy-start.20 = (f32[1024]{0:T(1024)S(1)}, f32[1024]{0:T(1024)}, u32[]{:S(2)}) copy-start(f32[1024]{0:T(1024)} %copy-done.19) | copy-start | bytes 12292
  746.0 23.5 %copy-start.23 = (f32[512]{0:T(512)S(1)}, f32[512]{0:T(512)}, u32[]{:S(2)}) copy-start(f32[512]{0:T(512)} %copy-done.22) | copy-start | bytes 6148
Sparse Core Ops, SparseCore 0:
  9.9 29.0 all-gather.10
  41.2 80.7 all-gather.8
  139.5 75.2 reduce-scatter.7
  216.7 29.5 all-gather.14
  248.4 80.7 all-gather.12
  331.1 27.5 all-gather.16
  360.7 29.3 all-gather.18
  391.7 80.7 all-gather.20
  505.9 75.2 reduce-scatter.11
  585.4 81.2 all-gather.22
  682.6 75.2 reduce-scatter.13
  760.2 78.3 reduce-scatter.9
  842.5 54.3 reduce-scatter.15
  901.2 53.8 reduce-scatter.17
  958.9 53.8 reduce-scatter.19
where the time goes:
time: 1030 us; the launch traced here: 1020 us
  waiting for transfers between devices  777 us (75%)
  matrix products  124 us (12%)
  blocking collectives  55.3 us (5%)
  other arithmetic  27.4 us (3%)
  between operations  14.5 us (1%)
  local copies, waits for them, and re-layouts  11.2 us (1%)
    all_gather x1, waiting for transfers between devices, body(): first_all = lax.all_gather(first, 'tensor', axis=0, tiled=True)  82.9 us
    all_gather x1, waiting for transfers between devices, body(): second_all = lax.all_gather(second, 'tensor', axis=0, tiled=True)  82.9 us
    all_gather x1, waiting for transfers between devices, body(): cot_all = lax.all_gather(d_out, 'tensor', axis=0, tiled=True)  82.4 us
    all_gather x1, waiting for transfers between devices, body(): lax.all_gather(d_resid.astype(jnp.bfloat16), 'tensor', axis=0, tiled=True)  81.4 us
    reduce_scatter x1, waiting for transfers between devices, body(): lax.psum_scatter((part_gate + part_up).astype(jnp.bfloat16), 'tensor', sc...  75.4 us
    reduce_scatter x1, waiting for transfers between devices, body(): lax.psum_scatter(jnp.dot(rows_now, out_full, preferred_element_type=jnp.f...  74.8 us
    reduce_scatter x1, waiting for transfers between devices, body(): lax.psum_scatter(grad_up, 'dp', scatter_dimension=0, tiled=True)  58.2 us
    reduce_scatter x1, waiting for transfers between devices, body(): lax.psum_scatter(grad_down, 'dp', scatter_dimension=1, tiled=True)  57.8 us
  transfers between devices with their start and end apart: 17, of which 16 were waited for; matrix products, arithmetic and copies ran while one was open for 9% of the time, Pallas kernels for 0%

commit v1 on v0

--- a/solution.py
+++ b/solution.py
@@ -149,7 +149,7 @@
         jnp.zeros((3, model_width), jnp.float32), taps_local, offset, 1
     )
     grad_gain1, grad_gain2, grad_conv = lax.psum(
-        (gain_one_part, gain_two_part, taps_whole), ("dp", "tensor")
+        lax.psum((gain_one_part, gain_two_part, taps_whole), "tensor"), "dp"
     )
     return (
         block_out,

time: 1030 us -> 1020 us (level)
    psum x1 -> x2, blocking collectives: 42.7 us -> 41 us  [the longest x1 23.3 us: body(): lax.psum(lax.psum((gain_one_part, gain_two_part, taps_whole), 'tensor'),...]
where the time goes in v1:
time: 1020 us
  waiting for transfers between devices  778 us (76%)
  matrix products  124 us (12%)
  blocking collectives  54.6 us (5%)
  other arithmetic  27.3 us (3%)
  between operations  14.5 us (1%)
    all_gather x1, waiting for transfers between devices, body(): first_all = lax.all_gather(first, 'tensor', axis=0, tiled=True)  82.9 us
    all_gather x1, waiting for transfers between devices, body(): second_all = lax.all_gather(second, 'tensor', axis=0, tiled=True)  82.9 us
    all_gather x1, waiting for transfers between devices, body(): cot_all = lax.all_gather(d_out, 'tensor', axis=0, tiled=True)  82.4 us
    all_gather x1, waiting for transfers between devices, body(): lax.all_gather(d_resid.astype(jnp.bfloat16), 'tensor', axis=0, tiled=True)  81.4 us
    reduce_scatter x1, waiting for transfers between devices, body(): lax.psum_scatter((part_gate + part_up).astype(jnp.bfloat16), 'tensor', sc...  75.4 us
    reduce_scatter x1, waiting for transfers between devices, body(): lax.psum_scatter(jnp.dot(rows_now, out_full, preferred_element_type=jnp.f...  74.8 us
    reduce_scatter x1, waiting for transfers between devices, body(): lax.psum_scatter(grad_up, 'dp', scatter_dimension=0, tiled=True)  58.2 us
    reduce_scatter x1, waiting for transfers between devices, body(): lax.psum_scatter(grad_down, 'dp', scatter_dimension=1, tiled=True)  57.8 us
  transfers between devices with their start and end apart: 17, of which 16 were waited for; matrix products, arithmetic and copies ran while one was open for 9% of the time, Pallas kernels for 0%

profile of v1, /device:TPU:0, one launch (start us, length us, event | category | flops | bytes accessed | tf_op | source)
XLA Modules:
  0.0 1019.0 jit_solution(11468530918710723090)
XLA Ops:
  8.6 1.5 fusion.26
  10.2 2.5 fusion.23
  13.5 13.6 %all_gather.29 = bf16[256,1024]{1,0:T(8,128)(2,1)} all-gather(bf16[256,128]{1,0:T(8,128)(2,1)S(1)} %copy-done.21), channel_id=1, replica_groups=mesh['dp'=8,'tensor'=4] {'dp'}, dimensions={1}, use_global_device_ids=true | all-gather | bytes 589824 | tf_op jit(solution)/shard_map/all_gather | solution.py:46
  27.1 12.3 %all-gather.11.cloned.1.call-done = bf16[1024,3,256]{2,0,1:T(8,128)(2,1)} async-done(((bf16[128,3,256]{2,0,1:T(8,128)(2,1)}), bf16[1024,3,256]{2,0,1:T(8,128)(2,1)}) %all-gather.11.cloned.1.call-update) | async-done | bytes 1572880 | tf_op jit(solution)/shard_map/all_gather | solution.py:45
  39.4 82.9 %all-gather.9.cloned.1.call-done = bf16[2048,1024]{1,0:T(8,128)(2,1)} async-done(((bf16[512,1024]{1,0:T(8,128)(2,1)}), bf16[2048,1024]{1,0:T(8,128)(2,1)}) %all-gather.9.cloned.1.call-update) | async-done | bytes 4194320 | tf_op jit(solution)/shard_map/all_gather | solution.py:60
  122.3 5.6 fusion.3
  128.4 2.2 copy-done.14
  133.2 2.1 multiply_convert_fusion.7
  135.3 3.3 convolution_convert_fusion.1
  139.4 74.8 %reduce-scatter.8.cloned.1.call-done = bf16[512,1024]{1,0:T(8,128)(2,1)} async-done(((bf16[2048,1024]{1,0:T(8,128)(2,1)}), bf16[512,1024]{1,0:T(8,128)(2,1)}) %reduce-scatter.8.cloned.1.call-update) | async-done | bytes 1048592 | tf_op jit(solution)/shard_map/reduce_scatter | solution.py:73
  214.2 1.7 multiply_reduce_fusion.2
  215.9 1.4 multiply_convert_fusion.6
  219.9 25.7 %all-gather.15.cloned.1.call-done = bf16[1024,1152]{1,0:T(8,128)(2,1)} async-done(((bf16[128,1152]{1,0:T(8,128)(2,1)}), bf16[1024,1152]{1,0:T(8,128)(2,1)}) %all-gather.15.cloned.1.call-update) | async-done | bytes 2359312 | tf_op jit(solution)/shard_map/all_gather | solution.py:47
  245.6 82.9 %all-gather.13.cloned.1.call-done = bf16[2048,1024]{1,0:T(8,128)(2,1)} async-done(((bf16[512,1024]{1,0:T(8,128)(2,1)}), bf16[2048,1024]{1,0:T(8,128)(2,1)}) %all-gather.13.cloned.1.call-update) | async-done | bytes 4194320 | tf_op jit(solution)/shard_map/all_gather | solution.py:82
  328.5 10.3 %fusion.39 = f32[2048,1152]{1,0:T(8,128)} fusion(bf16[2048,1024]{1,0:T(8,128)(2,1)} %all-gather.13.cloned.1.call-done, bf16[1024,1152]{1,0:T(8,128)(2,1)} %all-gather.15.cloned.1.call-done), kind=kOutput, calls=%fused_computation.77 | convolution fusion | flops 4831838208 | bytes 15990784 | tf_op jit(solution)/shard_map/dot_general | solution.py:83
  338.8 19.2 %all-gather.17.cloned.1.call-done = bf16[1024,1152]{1,0:T(8,128)(2,1)} async-done(((bf16[128,1152]{1,0:T(8,128)(2,1)}), bf16[1024,1152]{1,0:T(8,128)(2,1)}) %all-gather.17.cloned.1.call-update) | async-done | bytes 2359312 | tf_op jit(solution)/shard_map/all_gather | solution.py:48
  358.0 10.3 %fusion.40 = f32[2048,1152]{1,0:T(8,128)} fusion(bf16[2048,1024]{1,0:T(8,128)(2,1)} %all-gather.13.cloned.1.call-done, bf16[1024,1152]{1,0:T(8,128)(2,1)} %all-gather.17.cloned.1.call-done), kind=kOutput, calls=%fused_computation.78 | convolution fusion | flops 4831838208 | bytes 15990784 | tf_op jit(solution)/shard_map/dot_general | solution.py:84
  368.2 21.1 %all-gather.19.cloned.1.call-done = bf16[1152,1024]{1,0:T(8,128)(2,1)} async-done(((bf16[1152,128]{1,0:T(8,128)(2,1)}), bf16[1152,1024]{1,0:T(8,128)(2,1)}) %all-gather.19.cloned.1.call-update) | async-done | bytes 2359312 | tf_op jit(solution)/shard_map/all_gather | solution.py:49
  389.4 82.4 %all-gather.21.cloned.1.call-done = bf16[2048,1024]{1,0:T(8,128)(2,1)} async-done(((bf16[512,1024]{1,0:T(8,128)(2,1)}), bf16[2048,1024]{1,0:T(8,128)(2,1)}) %all-gather.21.cloned.1.call-update) | async-done | bytes 4194320 | tf_op jit(solution)/shard_map/all_gather | solution.py:96
  471.8 17.8 %multiply_convert_fusion = (bf16[2048,1152]{1,0:T(8,128)(2,1)}, bf16[2048,1152]{1,0:T(8,128)(2,1)}, bf16[2048,1152]{1,0:T(8,128)(2,1)}) fusion(f32[2048,1152]{1,0:T(8,128)} %fusion.39, f32[2048,1152]{1,0:T(8,128)} %fusion.40, bf16[2048,1024]{1,0:T(8,128)(2,1)} %all-gather.21.cloned.1.call-done, bf16[1152,1024]{1,0:T(8,128)(2,1)} %all-gather.19.cloned.1.call-done), kind=kOutput, calls=%fused_computation | convolution fusion | flops 4867227648 | bytes 39583744 | tf_op jit(solution)/shard_map/td,fd->tf/dot_general | solution.py:97
  489.7 7.7 fusion.41
  497.4 7.7 add_convert_fusion
  505.2 75.4 %reduce-scatter.12.cloned.1.call-done = bf16[512,1024]{1,0:T(8,128)(2,1)} async-done(((bf16[2048,1024]{1,0:T(8,128)(2,1)}), bf16[512,1024]{1,0:T(8,128)(2,1)}) %reduce-scatter.12.cloned.1.call-update) | async-done | bytes 1048592 | tf_op jit(solution)/shard_map/reduce_scatter | solution.py:110
  580.6 2.2 fusion.22
  582.8 1.8 fusion.35
  584.7 81.4 %all-gather.23.cloned.1.call-done = bf16[2048,1024]{1,0:T(8,128)(2,1)} async-done(((bf16[512,1024]{1,0:T(8,128)(2,1)}), bf16[2048,1024]{1,0:T(8,128)(2,1)}) %all-gather.23.cloned.1.call-update) | async-done | bytes 4194320 | tf_op jit(solution)/shard_map/all_gather | solution.py:115
  666.1 5.8 fusion.27
  676.8 5.0 bitcast_convert_fusion
  681.8 9.5 convolution_convert_fusion
  691.4 10.5 %fusion.42 = f32[1024,1152]{1,0:T(8,128)} fusion(bf16[2048,1024]{1,0:T(8,128)(2,1)} %all-gather.13.cloned.1.call-done, bf16[2048,1152]{1,0:T(8,128)(2,1)} %get-tuple-element.28), kind=kOutput, calls=%fused_computation.80 | convolution fusion | flops 4831838208 | bytes 13631488 | tf_op jit(solution)/shard_map/td,tf->df/dot_general | solution.py:101
  702.0 10.3 %fusion.43 = f32[1024,1152]{1,0:T(8,128)} fusion(bf16[2048,1024]{1,0:T(8,128)(2,1)} %all-gather.13.cloned.1.call-done, bf16[2048,1152]{1,0:T(8,128)(2,1)} %get-tuple-element.27), kind=kOutput, calls=%fused_computation.81 | convolution fusion | flops 4831838208 | bytes 13631488 | tf_op jit(solution)/shard_map/td,tf->df/dot_general | solution.py:102
  712.4 9.7 fusion.44
  722.2 3.8 fusion.32
  726.9 4.4 all-to-all-start.1
  731.3 6.7 fusion.29
  739.3 1.7 all-to-all-done.1
  741.1 4.3 all-to-all-start
  745.4 1.8 convert_reduce_fusion.1
  747.2 19.2 %all-to-all-done = bf16[8,128,3,256]{3,1,2,0:T(8,128)(2,1)} async-done(((bf16[8,128,3,256]{3,1,2,0:T(8,128)(2,1)}), bf16[8,128,3,256]{3,1,2,0:T(8,128)(2,1)}, u32[]{:S(2)}, u32[]{:S(2)}) %all-to-all-start) | async-done | bytes 1572896 | tf_op jit(solution)/shard_map/all_to_all | solution.py:17
  766.4 2.5 convert_reduce_fusion
  768.9 2.0 fusion.25
  770.9 17.7 %all-reduce.5 = (f32[3,1024]{1,0:T(4,128)S(1)}, f32[1024]{0:T(1024)S(1)}, f32[1024]{0:T(1024)S(1)}) all-reduce(f32[3,1024]{1,0:T(4,128)S(1)} %maximum_dynamic-update-slice_fusion, f32[1024]{0:T(1024)S(1)} %get-tuple-element.14, f32[1024]{0:T(1024)S(1)} %get-tuple-element.12), channel_id=1, replica_groups=mesh['dp'=8,'tensor'=4] {'tensor'}, use_global_device_ids=true, to_apply=%region_16.17 | all-reduce | flops 5120 | bytes 40960 | tf_op jit(solution)/shard_map/psum | solution.py:152
  788.7 23.3 %all-reduce.4 = (f32[3,1024]{1,0:T(4,128)}, f32[1024]{0:T(1024)}, f32[1024]{0:T(1024)}) all-reduce(f32[3,1024]{1,0:T(4,128)S(1)} %get-tuple-element.19, f32[1024]{0:T(1024)S(1)} %get-tuple-element.20, f32[1024]{0:T(1024)S(1)} %get-tuple-element.21), channel_id=1, replica_groups=mesh['dp'=8,'tensor'=4] {'dp'}, use_global_device_ids=true, to_apply=%region_17.18 | all-reduce | flops 5120 | bytes 40960 | tf_op jit(solution)/shard_map/psum | solution.py:151
  812.0 25.8 %reduce-scatter.10.cloned.1.call-done = bf16[512,1024]{1,0:T(8,128)(2,1)} async-done(((bf16[2048,1024]{1,0:T(8,128)(2,1)}), bf16[512,1024]{1,0:T(8,128)(2,1)}) %reduce-scatter.10.cloned.1.call-update) | async-done | bytes 1048592 | tf_op jit(solution)/shard_map/reduce_scatter | solution.py:89
  837.8 4.1 fusion.18
  842.0 54.3 %reduce-scatter.16.cloned.1.call-done = f32[128,1152]{1,0:T(8,128)} async-done(((f32[1024,1152]{1,0:T(8,128)}), f32[128,1152]{1,0:T(8,128)}) %reduce-scatter.16.cloned.1.call-update) | async-done | bytes 589840 | tf_op jit(solution)/shard_map/reduce_scatter | solution.py:104
  896.2 58.2 %reduce-scatter.18.cloned.1.call-done = f32[128,1152]{1,0:T(8,128)} async-done(((f32[1024,1152]{1,0:T(8,128)}), f32[128,1152]{1,0:T(8,128)}) %reduce-scatter.18.cloned.1.call-update) | async-done | bytes 589840 | tf_op jit(solution)/shard_map/reduce_scatter | solution.py:105
  954.4 57.8 %reduce-scatter.20.cloned.1.call-done = f32[1152,128]{1,0:T(8,128)} async-done(((f32[1152,1024]{1,0:T(8,128)}), f32[1152,128]{1,0:T(8,128)}) %reduce-scatter.20.cloned.1.call-update) | async-done | bytes 589840 | tf_op jit(solution)/shard_map/reduce_scatter | solution.py:106
  (105 shorter events, 16.1 us)
Async XLA Ops:
  7.2 32.2 %all-gather.11.cloned.1.call-start = ((), (), s32[]{:S(2)}) async-start(), calls=%async_computation.10 | async-start | bytes 1769472 | tf_op jit(solution)/shard_map/all_gather | solution.py:45
  7.9 114.4 %all-gather.9.cloned.1.call-start = ((), (), s32[]{:S(2)}) async-start(), calls=%async_computation.9 | async-start | bytes 5242880 | tf_op jit(solution)/shard_map/all_gather | solution.py:60
  8.6 4.8 copy-start.19
  8.6 4.8 copy-start.21
  10.2 112.1 %copy-start.22 = (f32[512]{0:T(512)}, f32[512]{0:T(512)S(1)}, u32[]{:S(2)}) copy-start(f32[512]{0:T(512)S(1)} %add_rsqrt_fusion.1) | copy-start | bytes 6148
  12.7 201.4 %reduce-scatter.8.cloned.1.call-start = ((), (), s32[]{:S(2)}) async-start(), calls=%async_computation.11 | async-start | bytes 5242880 | tf_op jit(solution)/shard_map/reduce_scatter | solution.py:73
  128.0 2.7 copy-start.14
  130.6 1.3 copy-start.2
  130.6 2.0 copy-start.6
  130.6 2.6 copy-start.8
  132.6 2.7 copy-start.4
  133.2 2.1 copy-start.15
  135.3 3.4 copy-start.13
  138.7 0.7 copy-start.24
  138.7 75.5 %copy-start = (bf16[512,1024]{1,0:T(8,128)(2,1)S(1)}, bf16[512,1024]{1,0:T(8,128)(2,1)}, u32[]{:S(2)}) copy-start(bf16[512,1024]{1,0:T(8,128)(2,1)} %param.10) | copy-start | bytes 3145732
  138.7 106.9 %all-gather.15.cloned.1.call-start = ((), (), s32[]{:S(2)}) async-start(), calls=%async_computation.13 | async-start | bytes 2654208 | tf_op jit(solution)/shard_map/all_gather | solution.py:47
  139.3 189.2 %all-gather.13.cloned.1.call-start = ((), (), s32[]{:S(2)}) async-start(), calls=%async_computation.12 | async-start | bytes 5242880 | tf_op jit(solution)/shard_map/all_gather | solution.py:82
  214.2 1.7 copy-start.1
  217.3 140.7 %all-gather.17.cloned.1.call-start = ((), (), s32[]{:S(2)}) async-start(), calls=%async_computation.14 | async-start | bytes 2654208 | tf_op jit(solution)/shard_map/all_gather | solution.py:48
  217.9 171.5 %all-gather.19.cloned.1.call-start = ((), (), s32[]{:S(2)}) async-start(), calls=%async_computation.15 | async-start | bytes 2654208 | tf_op jit(solution)/shard_map/all_gather | solution.py:49
  218.6 253.2 %all-gather.21.cloned.1.call-start = ((), (), s32[]{:S(2)}) async-start(), calls=%async_computation.17 | async-start | bytes 5242880 | tf_op jit(solution)/shard_map/all_gather | solution.py:96
  219.4 361.2 %reduce-scatter.12.cloned.1.call-start = ((), (), s32[]{:S(2)}) async-start(), calls=%async_computation.18 | async-start | bytes 5242880 | tf_op jit(solution)/shard_map/reduce_scatter | solution.py:110
  471.8 17.8 %copy-start.25 = (bf16[1024,1152]{1,0:T(8,128)(2,1)S(1)}, bf16[1024,1152]{1,0:T(8,128)(2,1)}, u32[]{:S(2)}) copy-start(bf16[1024,1152]{1,0:T(8,128)(2,1)} %all-gather.15.cloned.1.call-done) | copy-start | bytes 7077892
  489.7 7.7 copy-start.26
  489.7 7.7 copy-start.28
  505.1 77.7 %copy-start.10 = (bf16[512,1024]{1,0:T(8,128)(2,1)S(1)}, bf16[512,1024]{1,0:T(8,128)(2,1)}, u32[]{:S(2)}) copy-start(bf16[512,1024]{1,0:T(8,128)(2,1)} %param.19) | copy-start | bytes 3145732
  505.1 160.9 %all-gather.23.cloned.1.call-start = ((), (), s32[]{:S(2)}) async-start(), calls=%async_computation.19 | async-start | bytes 5242880 | tf_op jit(solution)/shard_map/all_gather | solution.py:115
  580.6 2.2 copy-start.11
  584.6 184.3 %reduce-scatter.14.cloned.1.call-start = ((), (), s32[]{:S(2)}) async-start(), calls=%async_computation.20 | async-start | bytes 5242880 | tf_op jit(solution)/shard_map/reduce_scatter | solution.py:137
  666.1 5.8 copy-start.5
  666.1 5.8 copy-start.9
  666.1 6.0 copy-start.12
  672.1 1.6 copy-start.3
  672.9 2.8 copy-start.16
  673.7 1.6 copy-start.7
  674.4 1.3 copy-start.18
  675.3 1.5 copy-start.27
  675.7 1.0 copy-start.17
  681.8 156.0 %reduce-scatter.10.cloned.1.call-start = ((), (), s32[]{:S(2)}) async-start(), calls=%async_computation.16 | async-start | bytes 5242880 | tf_op jit(solution)/shard_map/reduce_scatter | solution.py:89
  691.3 204.9 %reduce-scatter.16.cloned.1.call-start = ((), (), s32[]{:S(2)}) async-start(), calls=%async_computation.21 | async-start | bytes 5308416 | tf_op jit(solution)/shard_map/reduce_scatter | solution.py:104
  701.9 252.5 %reduce-scatter.18.cloned.1.call-start = ((), (), s32[]{:S(2)}) async-start(), calls=%async_computation.22 | async-start | bytes 5308416 | tf_op jit(solution)/shard_map/reduce_scatter | solution.py:105
  712.4 299.9 %reduce-scatter.20.cloned.1.call-start = ((), (), s32[]{:S(2)}) async-start(), calls=%async_computation.23 | async-start | bytes 5308416 | tf_op jit(solution)/shard_map/reduce_scatter | solution.py:106
  726.9 14.2 %all-to-all-start.1 = ((bf16[8,256,128]{2,1,0:T(8,128)(2,1)}), bf16[8,256,128]{2,1,0:T(8,128)(2,1)}, u32[]{:S(2)}, u32[]{:S(2)}) async-start(bf16[8,256,128]{2,1,0:T(8,128)(2,1)} %bitcast.76), calls=%async_computation.5 | async-start | bytes 1048576 | tf_op jit(solution)/shard_map/all_to_all | solution.py:17
  741.1 25.4 %all-to-all-start = ((bf16[8,128,3,256]{3,1,2,0:T(8,128)(2,1)}), bf16[8,128,3,256]{3,1,2,0:T(8,128)(2,1)}, u32[]{:S(2)}, u32[]{:S(2)}) async-start(bf16[8,128,3,256]{3,1,2,0:T(8,128)(2,1)} %copy.22), calls=%async_computation.4 | async-start | bytes 3145728 | tf_op jit(solution)/shard_map/all_to_all | solution.py:17
  745.4 23.5 %copy-start.20 = (f32[1024]{0:T(1024)S(1)}, f32[1024]{0:T(1024)}, u32[]{:S(2)}) copy-start(f32[1024]{0:T(1024)} %copy-done.19) | copy-start | bytes 12292
  745.4 23.5 %copy-start.23 = (f32[512]{0:T(512)S(1)}, f32[512]{0:T(512)}, u32[]{:S(2)}) copy-start(f32[512]{0:T(512)} %copy-done.22) | copy-start | bytes 6148
Sparse Core Ops, SparseCore 0:
  9.9 29.4 all-gather.10
  41.5 80.7 all-gather.8
  138.8 75.2 reduce-scatter.7
  216.0 29.5 all-gather.14
  247.7 80.7 all-gather.12
  330.4 27.5 all-gather.16
  360.0 29.3 all-gather.18
  391.0 80.7 all-gather.20
  505.3 75.2 reduce-scatter.11
  584.8 81.2 all-gather.22
  681.9 75.2 reduce-scatter.13
  759.5 78.3 reduce-scatter.9
  841.9 54.3 reduce-scatter.15
  900.5 53.8 reduce-scatter.17
  958.3 53.8 reduce-scatter.19
